TPU v7x, 32 devices: a whole 2x2x4 slice. The times are simulated.
32 devices in a mesh: shard: 4 (over z), context: 2 (over x), tensor: 4 (over y, core).
Axes of the slice: x: 2, y: 2, z: 4, core: 2. Of those that a mesh axis runs over, the one named last changes fastest.
Arguments:
- hidden_in: bfloat16 [4, 2048, 1536], P('shard', 'context'), may hold values from -6 to 6
- norm_gain: float32 [1536], replicated, may hold values from 0.5 to 1.5
- w_in_zx: bfloat16 [1536, 2, 3072], P('shard', None, 'tensor'), may hold values from -0.15625 to 0.15625
- w_in_bc: bfloat16 [1536, 256], P('shard'), may hold values from -0.15625 to 0.15625
- w_in_dt: bfloat16 [1536, 48], P('shard', 'tensor'), may hold values from -0.15625 to 0.15625
- conv_x: float32 [5, 3072], P(None, 'tensor'), may hold values from -3 to 3
- conv_bc: float32 [5, 256], replicated, may hold values from -3 to 3
- dt_bias: float32 [48], P('tensor'), may hold values from -6 to -2.5
- a_log: float32 [48], P('tensor'), may hold values from -1 to 1.5
- d_skip: float32 [48], P('tensor'), may hold values from 0.5 to 1.5
- out_gain: float32 [3072], P('tensor'), may hold values from 0.5 to 1.5
- w_out: bfloat16 [3072, 1536], P('tensor', 'shard'), may hold values from -0.109375 to 0.109375
- cotangent: bfloat16 [4, 2048, 1536], P('shard', 'context'), may hold values from -6 to 6
Outputs:
- out: bfloat16 [4, 2048, 1536], P('shard', 'context')
- grad_in: float32 [4, 2048, 1536], P('shard', 'context')
- grad_norm_gain: float32 [1536], replicated
- grad_w_in_zx: float32 [1536, 2, 3072], P(('shard', 'context'), None, 'tensor')
- grad_w_in_bc: float32 [1536, 256], P(('shard', 'context'))
- grad_w_in_dt: float32 [1536, 48], P(('shard', 'context'), 'tensor')
- grad_conv_x: float32 [5, 3072], P(None, 'tensor')
- grad_conv_bc: float32 [5, 256], replicated
- grad_dt_bias: float32 [48], P('tensor')
- grad_a_log: float32 [48], P('tensor')
- grad_d_skip: float32 [48], P('tensor')
- grad_out_gain: float32 [3072], P('tensor')
- grad_w_out: float32 [3072, 1536], P('tensor', ('shard', 'context'))
- rms_stream: float32 [], replicated
- rms_mixer: float32 [], replicated
All inputs are finite; a program needn't handle non-finite values.
Results may differ from a plain program's by a relative error of at most 0.012.
Values may be sent and summed in bfloat16 or wider, within the bound.
No kernel may reach another device: no remote copies, remote signals or barrier semaphores. Data moves between devices by JAX's collectives and lax.ppermute only.
A program may use at most 192 MiB of HBM per device.

v0:
```python
import jax
import jax.numpy as jnp
from jax import lax
from jax.sharding import PartitionSpec as P

CH = 256
EPSILON = 1e-05
PRECISE = lax.Precision.HIGHEST


def shifted(array, axis, by):
    length = lax.axis_size(axis)
    pairs = [(i, i + by) for i in range(length) if 0 <= i + by < length]
    return lax.ppermute(array, axis, pairs)


def carried_in(array, axis, combine, identity, reverse):
    length, place = (lax.axis_size(axis), lax.axis_index(axis))
    everything = jax.tree.map(lambda part: lax.all_gather(part, axis), array)
    start = jax.tree.map(
        lambda part, zero: jnp.broadcast_to(jnp.asarray(zero, part.dtype), part.shape),
        array,
        identity,
    )

    def hop(k, before):
        at = length - 1 - k if reverse else k
        reached = at > place if reverse else at < place
        new = combine(before, jax.tree.map(lambda part: part[at], everything))
        return jax.tree.map(lambda a, b: jnp.where(reached, a, b), new, before)

    return lax.fori_loop(0, length, hop, start)


def combine_states(earlier, nearer):
    return (earlier[0] * nearer[0], nearer[0][..., None, None] * earlier[1] + nearer[1])


def silu_grad(values, sigmoid_val):
    return sigmoid_val * (1.0 + values * (1.0 - sigmoid_val))


def contract_rows(left_op, right_op):
    return lax.dot_general(
        left_op, right_op, (((0,), (0,)), ((), ())), preferred_element_type=jnp.float32
    )


def contract_cols(left_op, right_op):
    return lax.dot_general(
        left_op, right_op, (((1,), (1,)), ((), ())), preferred_element_type=jnp.float32
    )


def reverse_cumsum(values, axis_num):
    return jnp.flip(jnp.cumsum(jnp.flip(values, axis_num), axis=axis_num), axis_num)


def advance(running, element):
    return (element[0][..., None, None] * running + element[1], running)


def retreat(running, element):
    return (element[1] + element[0][..., None, None] * running, running)


def on_device(
    hidden_in,
    norm_gain,
    w_in_zx,
    w_in_bc,
    w_in_dt,
    conv_x,
    conv_bc,
    dt_bias,
    a_log,
    d_skip,
    out_gain,
    w_out,
    cotangent,
):
    seq_count, local_len, model_dim = hidden_in.shape
    inner_dev = w_in_zx.shape[2]
    heads_dev = w_in_dt.shape[1]
    head_dim = inner_dev // heads_dev
    state_dim = w_in_bc.shape[1] // 2
    tap_count = conv_x.shape[0] - 1
    inner_all = inner_dev * lax.axis_size("tensor")
    block_len = CH
    block_count = local_len // block_len
    row_count = seq_count * local_len
    channels = inner_dev + 2 * state_dim
    zx_full, bc_full, dt_full, out_full = (
        lax.all_gather(w_in_zx, "shard", axis=0, tiled=True),
        lax.all_gather(w_in_bc, "shard", axis=0, tiled=True),
        lax.all_gather(w_in_dt, "shard", axis=0, tiled=True),
        lax.all_gather(w_out, "shard", axis=1, tiled=True),
    )
    zx_mat = zx_full.reshape(model_dim, 2 * inner_dev)
    stream_in = hidden_in.reshape(row_count, model_dim).astype(jnp.float32)
    scale_in = lax.rsqrt(jnp.mean(stream_in * stream_in, axis=-1, keepdims=True) + EPSILON)
    normed = (stream_in * scale_in * norm_gain).astype(jnp.bfloat16)
    zx_val = jnp.dot(normed, zx_mat, preferred_element_type=jnp.float32)
    gate_val = zx_val[:, :inner_dev]
    bc_val = jnp.dot(normed, bc_full, preferred_element_type=jnp.float32)
    dt_raw = jnp.dot(normed, dt_full, preferred_element_type=jnp.float32)
    pre_conv = jnp.concatenate([zx_val[:, inner_dev:], bc_val], axis=-1).reshape(
        seq_count, local_len, channels
    )
    prev_rows = shifted(pre_conv[:, local_len - tap_count + 1 :], "context", 1)
    padded = jnp.concatenate([prev_rows, pre_conv], axis=1)
    conv_all = jnp.concatenate([conv_x, conv_bc], axis=1)
    conv_out = conv_all[tap_count] + conv_all[0] * padded[:, 0:local_len]
    for tap_idx in range(1, tap_count):
        conv_out = conv_out + conv_all[tap_idx] * padded[:, tap_idx : tap_idx + local_len]
    sig_conv = jax.nn.sigmoid(conv_out)
    activated = (conv_out * sig_conv).astype(jnp.bfloat16)
    xa_blk = activated[..., :inner_dev].reshape(
        seq_count, block_count, block_len, heads_dev, head_dim
    )
    bm_blk = activated[..., inner_dev : inner_dev + state_dim].reshape(
        seq_count, block_count, block_len, state_dim
    )
    cm_blk = activated[..., inner_dev + state_dim :].reshape(
        seq_count, block_count, block_len, state_dim
    )
    xa_f = xa_blk.astype(jnp.float32)
    bm_f = bm_blk.astype(jnp.float32)
    cm_f = cm_blk.astype(jnp.float32)
    dt_pre = dt_raw + dt_bias
    dt_val = jax.nn.softplus(dt_pre)
    rate_neg = -jnp.exp(a_log)
    dt_q = dt_val.reshape(seq_count, block_count, block_len, heads_dev)
    log_q = (dt_val * rate_neg).reshape(seq_count, block_count, block_len, heads_dev)
    cum_q = jnp.cumsum(log_q, axis=2)
    block_log = cum_q[:, :, -1]
    cum_t = jnp.swapaxes(cum_q, 2, 3)
    dt_t = jnp.swapaxes(dt_q, 2, 3)
    positions = jnp.arange(block_len)
    lower_mask = positions[:, None] >= positions[None, :]
    log_gap = cum_t[..., :, None] - cum_t[..., None, :]
    decay_mat = jnp.exp(jnp.where(lower_mask, log_gap, 0.0)) * lower_mask.astype(jnp.float32)
    scores = jnp.einsum("scin,scjn->scij", cm_blk, bm_blk, preferred_element_type=jnp.float32)
    weights_f = scores[:, :, None] * decay_mat * dt_t[..., None, :]
    weights_b = weights_f.astype(jnp.bfloat16)
    y_intra = jnp.einsum(
        "schij,scjhp->scihp", weights_b, xa_blk, preferred_element_type=jnp.float32
    )
    w_end = jnp.exp(block_log[:, :, None, :] - cum_q) * dt_q
    xw_val = (xa_f * w_end[..., None]).astype(jnp.bfloat16)
    state_add = jnp.einsum("scjn,scjhp->schnp", bm_blk, xw_val, preferred_element_type=jnp.float32)
    block_decay = jnp.exp(block_log)
    zero_state = jnp.zeros((seq_count, heads_dev, state_dim, head_dim), jnp.float32)
    end_local, start_local = lax.scan(
        advance, zero_state, (jnp.moveaxis(block_decay, 1, 0), jnp.moveaxis(state_add, 1, 0))
    )
    start_local = jnp.moveaxis(start_local, 0, 1)
    dev_decay = jnp.prod(block_decay, axis=1)
    _, in_state = carried_in(
        (dev_decay, end_local),
        "context",
        combine_states,
        (jnp.ones_like(dev_decay), jnp.zeros_like(end_local)),
        False,
    )
    before_dec = jnp.exp(jnp.cumsum(block_log, axis=1) - block_log)
    start_state = start_local + before_dec[..., None, None] * in_state[:, None]
    start_b = start_state.astype(jnp.bfloat16)
    cum_exp = jnp.exp(cum_q)
    cm_scaled = (cm_f[:, :, :, None, :] * cum_exp[..., None]).astype(jnp.bfloat16)
    y_inter = jnp.einsum(
        "scihn,schnp->scihp", cm_scaled, start_b, preferred_element_type=jnp.float32
    )
    y_ssd = (y_intra + y_inter + d_skip[:, None] * xa_f).reshape(row_count, inner_dev)
    sig_gate = jax.nn.sigmoid(gate_val)
    silu_gate = gate_val * sig_gate
    gated = y_ssd * silu_gate
    square_sum = lax.psum(jnp.sum(gated * gated, axis=-1), "tensor")
    scale_out = lax.rsqrt(square_sum / inner_all + EPSILON)[:, None]
    out_in = (gated * scale_out * out_gain).astype(jnp.bfloat16)
    mixed = lax.psum(jnp.dot(out_in, out_full, preferred_element_type=jnp.float32), "tensor")
    stream = stream_in + mixed
    stream_sq = jnp.sum(stream * stream)
    mixed_sq = jnp.sum(mixed * mixed)
    grad_rows = cotangent.reshape(row_count, model_dim)
    grad_stream = grad_rows.astype(jnp.float32)
    grad_wout = contract_rows(out_in, grad_rows)
    wout_share = lax.psum_scatter(grad_wout, ("shard", "context"), scatter_dimension=1, tiled=True)
    grad_on = contract_cols(grad_rows, out_full)
    grad_og = jnp.sum(grad_on * gated * scale_out, axis=0)
    grad_gn = grad_on * out_gain
    dot_sum = lax.psum(jnp.sum(grad_gn * gated, axis=-1), "tensor")
    grad_gated = scale_out * grad_gn - gated * scale_out**3 * (dot_sum / inner_all)[:, None]
    grad_y = (grad_gated * silu_gate).astype(jnp.bfloat16)
    grad_gate = (grad_gated * y_ssd * silu_grad(gate_val, sig_gate)).astype(jnp.bfloat16)
    grad_yb = grad_y.reshape(seq_count, block_count, block_len, heads_dev, head_dim)
    grad_yf = grad_yb.astype(jnp.float32)
    grad_wts = jnp.einsum("scihp,scjhp->schij", grad_yb, xa_blk, preferred_element_type=jnp.float32)
    grad_xa = (
        jnp.einsum("schij,scihp->scjhp", weights_b, grad_yb, preferred_element_type=jnp.float32)
        + d_skip[:, None] * grad_yf
    )
    grad_skip = jnp.sum(grad_yf * xa_f, axis=(0, 1, 2, 4))
    weighted = grad_wts * weights_f
    grad_cum_t = jnp.sum(weighted, axis=-1) - jnp.sum(weighted, axis=-2)
    grad_dt_t = jnp.sum(grad_wts * scores[:, :, None] * decay_mat, axis=-2)
    grad_scores = jnp.sum(grad_wts * decay_mat * dt_t[..., None, :], axis=2)
    grad_bm = jnp.einsum("scij,scin->scjn", grad_scores, cm_f, precision=PRECISE)
    grad_cm = jnp.einsum("scij,scjn->scin", grad_scores, bm_f, precision=PRECISE)
    grad_scaled = jnp.einsum(
        "scihp,schnp->scihn", grad_yb, start_b, preferred_element_type=jnp.float32
    )
    grad_cm = grad_cm + jnp.sum(grad_scaled * cum_exp[..., None], axis=3)
    grad_cum_q = (
        jnp.swapaxes(grad_cum_t, 2, 3)
        + jnp.sum(grad_scaled * cm_f[:, :, :, None, :], axis=-1) * cum_exp
    )
    grad_start = jnp.einsum(
        "scihn,scihp->schnp", cm_scaled, grad_yb, preferred_element_type=jnp.float32
    )
    gin_local, after_local = lax.scan(
        retreat,
        zero_state,
        (jnp.moveaxis(block_decay, 1, 0), jnp.moveaxis(grad_start, 1, 0)),
        reverse=True,
    )
    after_local = jnp.moveaxis(after_local, 0, 1)
    _, grad_end = carried_in(
        (dev_decay, gin_local),
        "context",
        combine_states,
        (jnp.ones_like(dev_decay), jnp.zeros_like(gin_local)),
        True,
    )
    after_dec = jnp.exp(jnp.sum(block_log, axis=1, keepdims=True) - jnp.cumsum(block_log, axis=1))
    grad_after = after_local + after_dec[..., None, None] * grad_end[:, None]
    grad_lam = block_decay * jnp.sum(grad_after * start_state, axis=(-2, -1))
    grad_after_b = grad_after.astype(jnp.bfloat16)
    grad_xw = jnp.einsum(
        "scjn,schnp->scjhp", bm_blk, grad_after_b, preferred_element_type=jnp.float32
    )
    grad_bm = grad_bm + jnp.einsum(
        "scjhp,schnp->scjn", xw_val, grad_after_b, preferred_element_type=jnp.float32
    )
    grad_xa = grad_xa + grad_xw * w_end[..., None]
    grad_wend = jnp.sum(grad_xw * xa_f, axis=-1)
    grad_cum_q = grad_cum_q - grad_wend * w_end
    grad_lam = grad_lam + jnp.sum(grad_wend * w_end, axis=2)
    grad_dt_q = jnp.swapaxes(grad_dt_t, 2, 3) + grad_wend * jnp.exp(
        block_log[:, :, None, :] - cum_q
    )
    grad_log = reverse_cumsum(grad_cum_q, 2) + grad_lam[:, :, None, :]
    grad_dt_q = grad_dt_q + grad_log * rate_neg
    grad_alog = jnp.sum(grad_log * log_q, axis=(0, 1, 2))
    grad_raw = grad_dt_q.reshape(row_count, heads_dev) * jax.nn.sigmoid(dt_pre)
    grad_dtb = jnp.sum(grad_raw, axis=0)
    bc_part = jnp.concatenate([grad_bm, grad_cm], axis=-1).reshape(row_count, 2 * state_dim)
    bc_sum = lax.psum(bc_part, "tensor")
    grad_act = jnp.concatenate(
        [
            grad_xa.reshape(seq_count, local_len, inner_dev),
            bc_sum.reshape(seq_count, local_len, 2 * state_dim),
        ],
        axis=-1,
    )
    grad_conv = grad_act * silu_grad(conv_out, sig_conv)
    next_rows = shifted(grad_conv[:, : tap_count - 1], "context", -1)
    extended = jnp.concatenate([grad_conv, next_rows], axis=1)
    grad_pre = conv_all[0] * extended[:, tap_count - 1 : tap_count - 1 + local_len]
    for tap_idx in range(1, tap_count):
        start_at = tap_count - 1 - tap_idx
        grad_pre = grad_pre + conv_all[tap_idx] * extended[:, start_at : start_at + local_len]
    taps_grad = [
        jnp.sum(grad_conv * padded[:, tap_idx : tap_idx + local_len], axis=(0, 1))
        for tap_idx in range(tap_count)
    ]
    grad_taps = jnp.stack(taps_grad + [jnp.sum(grad_conv, axis=(0, 1))], axis=0)
    grad_pre_rows = grad_pre.reshape(row_count, channels)
    grad_zx = jnp.concatenate(
        [grad_gate, grad_pre_rows[:, :inner_dev].astype(jnp.bfloat16)], axis=-1
    )
    grad_bc = grad_pre_rows[:, inner_dev:].astype(jnp.bfloat16)
    grad_raw_b = grad_raw.astype(jnp.bfloat16)
    grad_wzx = contract_rows(normed, grad_zx).reshape(model_dim, 2, inner_dev)
    grad_wbc = contract_rows(normed, grad_bc)
    grad_wdt = contract_rows(normed, grad_raw_b)
    part_in = contract_cols(grad_zx, zx_mat) + contract_cols(grad_raw_b, dt_full)
    grad_normed = lax.psum(part_in, "tensor") + contract_cols(grad_bc, bc_full)
    grad_ng = jnp.sum(grad_normed * stream_in * scale_in, axis=0)
    grad_un = grad_normed * norm_gain
    grad_input = (
        grad_stream
        + scale_in * grad_un
        - stream_in * scale_in**3 * jnp.mean(grad_un * stream_in, axis=-1, keepdims=True)
    )
    summed = lax.psum(
        (
            grad_ng,
            grad_taps[:, :inner_dev],
            grad_taps[:, inner_dev:],
            grad_dtb,
            grad_alog,
            grad_skip,
            grad_og,
            jnp.stack([stream_sq, mixed_sq]),
        ),
        ("shard", "context"),
    )
    zx_share, bc_share, dt_share = (
        lax.psum_scatter(grad_wzx, ("shard", "context"), scatter_dimension=0, tiled=True),
        lax.psum_scatter(grad_wbc, ("shard", "context"), scatter_dimension=0, tiled=True),
        lax.psum_scatter(grad_wdt, ("shard", "context"), scatter_dimension=0, tiled=True),
    )
    entry_count = row_count * model_dim * lax.axis_size("shard") * lax.axis_size("context")
    square_totals = summed[7]
    return (
        stream.astype(jnp.bfloat16).reshape(hidden_in.shape),
        grad_input.reshape(hidden_in.shape),
        summed[0],
        zx_share,
        bc_share,
        dt_share,
        summed[1],
        summed[2],
        summed[3],
        summed[4],
        summed[5],
        summed[6],
        wout_share,
        jnp.sqrt(square_totals[0] / entry_count),
        jnp.sqrt(square_totals[1] / entry_count),
    )


def solution(mesh):
    placed = (
        P("shard", "context", None),
        P(),
        P("shard", None, "tensor"),
        P("shard", None),
        P("shard", "tensor"),
        P(None, "tensor"),
        P(),
        P("tensor"),
        P("tensor"),
        P("tensor"),
        P("tensor"),
        P("tensor", "shard"),
        P("shard", "context", None),
    )
    return jax.shard_map(
        on_device,
        mesh=mesh,
        in_specs=placed,
        out_specs=(
            P("shard", "context", None),
            P("shard", "context", None),
            P(),
            P(("shard", "context"), None, "tensor"),
            P(("shard", "context"), None),
            P(("shard", "context"), "tensor"),
            P(None, "tensor"),
            P(),
            P("tensor"),
            P("tensor"),
            P("tensor"),
            P("tensor"),
            P("tensor", ("shard", "context")),
            P(),
            P(),
        ),
        check_vma=False,
    )
```

profile of v0, /device:TPU:0, one launch (start us, length us, event | category | flops | bytes accessed | tf_op | source)
XLA Modules:
  0.0 1050.1 jit_solution(12844477060453908155)
XLA Ops:
  8.8 2.7 fusion.14
  12.1 15.0 %all_gather.34 = bf16[1536,12]{0,1:T(8,128)(2,1)S(1)} all-gather(bf16[384,12]{0,1:T(8,128)(2,1)S(1)} %copy-done.75), channel_id=1, replica_groups=mesh['shard'=4,'context'=2,'tensor'=4] {'shard'}, dimensions={0}, use_global_device_ids=true | all-gather | bytes 46080 | tf_op jit(solution)/shard_map/all_gather | solution.py:96
  32.2 29.5 %all_gather.33 = bf16[1536,256]{1,0:T(8,128)(2,1)S(1)} all-gather(bf16[384,256]{1,0:T(8,128)(2,1)} %param.24), channel_id=1, replica_groups=mesh['shard'=4,'context'=2,'tensor'=4] {'shard'}, dimensions={0}, use_global_device_ids=true | all-gather | bytes 983040 | tf_op jit(solution)/shard_map/all_gather | solution.py:95
  68.2 46.2 %all-gather.6.cloned.1.call-done = bf16[1536,2,768]{2,1,0:T(2,128)(2,1)} async-done(((bf16[384,2,768]{2,1,0:T(2,128)(2,1)}), bf16[1536,2,768]{2,1,0:T(2,128)(2,1)}) %all-gather.6.cloned.1.call-update) | async-done | bytes 4718608 | tf_op jit(solution)/shard_map/all_gather | solution.py:94
  114.4 3.4 copy.488
  117.8 5.1 fusion.61
  129.0 3.4 collective-permute-start
  140.0 5.4 all-reduce
  151.0 10.0 multiply_convert_fusion.3
  161.0 2.9 fusion.125
  164.7 2.7 copy.402
  167.4 3.9 reshape.673
  171.3 3.1 convolution_bitcast_fusion
  176.4 12.2 %while.60 = (s32[]{:T(128)}, f32[1,12,128,64]{3,2,1,0:T(8,128)S(1)}, f32[4,1,12,128,64]{4,3,2,1,0:T(8,128)}, f32[4,1,12]{2,1,0:T(1,128)}, f32[4,1,12,128,64]{3,4,2,0,1:T(8,128)}, /*index=5*/s32[]{:T(128)}, s32[]{:T(128)}) while((s32[]{:T(128)}, f32[1,12,128,64]{3,2,1,0:T(8,128)S(1)}, f32[4,1,12,128,64]{4,3,2,1,0:T(8,128)}, ...), condition=%wide.region_4.5_spmd.clone, body=%wide.region_3.4_spmd.clone.sunk | while | flops 393219 | bytes 3932912 | solution.py:154
  192.9 3.6 copy.426
  196.5 5.2 reshape.700
  201.7 10.5 %all-gather.1 = f32[2,12,128,64]{2,3,1,0:T(8,128)} all-gather(f32[1,12,128,64]{2,3,1,0:T(8,128)S(1)} %copy.421), channel_id=3, replica_groups=mesh['shard'=4,'context'=2,'tensor'=4] {'context'}, dimensions={0}, use_global_device_ids=true | all-gather | bytes 1179648 | tf_op jit(solution)/shard_map/all_gather | solution.py:19
  212.2 6.7 fusion.32
  218.9 4.3 while.61
  223.2 6.2 bitcast_add_fusion.5
  231.5 2.4 copy.489
  233.9 3.6 copy.429
  237.5 5.4 multiply_reduce_fusion.10
  242.9 5.6 psum.91
  248.5 8.6 multiply_reduce_fusion.8
  257.1 6.7 psum.93
  263.9 8.0 fusion.52
  271.9 2.6 copy.431
  274.5 3.2 copy.433
  277.7 3.9 reshape.688
  281.5 4.4 fusion.73
  288.0 12.2 %while.62 = (s32[]{:T(128)}, f32[1,12,128,64]{3,2,1,0:T(8,128)S(1)}, f32[4,1,12,128,64]{4,3,2,1,0:T(8,128)}, f32[4,1,12,128,64]{3,4,2,0,1:T(8,128)}, f32[4,1,12]...) while((s32[]{:T(128)}, f32[1,12,128,64]{3,2,1,0:T(8,128)S(1)}, ...), condition=%wide.region_15.16_spmd.clone, body=%wide.region_14.15_spmd.clone.sunk | while | flops 393220 | bytes 3932424 | solution.py:221
  300.5 10.7 %all-gather.2 = f32[2,12,128,64]{2,3,1,0:T(8,128)S(1)} all-gather(f32[1,12,128,64]{2,3,1,0:T(8,128)S(1)} %copy.438), channel_id=4, replica_groups=mesh['shard'=4,'context'=2,'tensor'=4] {'context'}, dimensions={0}, use_global_device_ids=true | all-gather | bytes 1179648 | tf_op jit(solution)/shard_map/all_gather | solution.py:19
  313.5 3.5 fusion.55
  318.9 4.0 fusion.77
  323.0 11.9 %fusion.12 = (f32[4,12,256]{2,1,0:T(8,128)}, f32[4,12,256]{2,1,0:T(8,128)}, f32[4,12,256]{2,1,0:T(8,128)}, f32[4,256,256]{2,1,0:T(8,128)}) fusion(f32[4,12,256]{2,1,0:T(8,128)S(1)} %copy-done.61, f32[256,256]{1,0:T(8,128)S(1)} %copy-done.46, f32[4,12,256]{2,1,0:T(8,128)S(1)} %copy-done.59, f32[4,256,256]{2,1,0:T(8,128)S(1)} %copy-done.33, ...), kind=kOutput, calls=%fused_computation.32 | convolution fusion | flops 446394368 | bytes 5816320 | tf_op jit(solution)/shard_map/scihp,scjhp->schij/dot_general | solution.py:198
  335.1 3.9 fusion.54
  340.8 2.4 fusion.26
  349.4 5.1 reduce-window.16
  357.5 2.9 reshape.701
  360.4 7.3 fusion.51
  369.8 3.0 reshape.689
  372.8 3.7 copy.451
  390.7 25.7 %all-reduce.6.cloned.1.call-done = f32[1,1024,256]{2,1,0:T(8,128)} async-done(((f32[1,1024,256]{2,1,0:T(8,128)}), f32[1,1024,256]{2,1,0:T(8,128)}) %all-reduce.6.cloned.1.call-update) | async-done | bytes 1048592 | tf_op jit(solution)/shard_map/psum | solution.py:258
  416.4 11.7 %fusion.119 = (f32[1024]{0:T(1024)S(1)}, f32[1024]{0:T(1024)S(1)}, f32[1024]{0:T(1024)S(1)}, f32[1024]{0:T(1024)S(1)}, f32[1024]{0:T(1024)S(1)}, /*index=5*/f32[1,1024,1024]{2,1,0:T(8,128)S(1)}) fusion(f32[1024,256]{1,0:T(8,128)} %fusion.129, f32[1024,768]{1,0:T(8,128)} %copy-done.9, f32[1,1024,1024]{2,1,0:T(8,128)} %copy-done.7, ...), kind=kLoop, calls=%fused_computation.207 | loop fusion | flops 23063552 | bytes 21004288 | tf_op jit(solution)/shard_map/reduce_sum | solution.py:277
  429.7 5.1 fusion.118
  440.4 5.1 fusion.70
  445.5 3.7 convolution_add_fusion.1
  449.3 3.8 fusion.69
  453.1 4.7 copy.481
  457.8 10.5 fusion.49
  468.3 3.2 fusion.92
  471.8 7.7 fusion.56
  480.4 2.8 reduce-scatter.13.cloned.1.call-done
  484.9 221.3 %all-reduce.8.cloned.1.call-done = (f32[1024,1536]{1,0:T(8,128)}, f32[1024,1536]{1,0:T(8,128)}) async-done(((f32[1024,1536]{1,0:T(8,128)}, f32[1024,1536]{1,0:T(8,128)}), (f32[1024,1536]{1,0:T(8,128)}, f32[1024,1536]{1,0:T(8,128)})) %all-reduce.8.cloned.1.call-update) | async-done | bytes 12582928 | tf_op jit(solution)/shard_map/psum | solution.py:181
  706.1 4.3 convolution_add_fusion
  710.5 2.9 copy-done.18
  713.4 5.9 multiply_reduce_fusion.3
  720.7 41.1 %all-reduce.1 = (f32[1536]{0:T(1024)}, f32[5,768]{1,0:T(8,128)}, f32[5,256]{1,0:T(8,128)}, f32[12]{0:T(128)}, f32[12]{0:T(128)}, /*index=5*/f32[12]{0:T(128)}, f32[768]{0:T(1024)}, f32[2]{0:T(128)S(1)}) all-reduce(f32[1536]{0:T(1024)S(1)} %get-tuple-element.717, ...), channel_id=1, replica_groups=mesh['shard'=4,'context'=2,'tensor'=4] {'shard','context'}, use_global_device_ids=true, to_apply=%region_34.35 | all-reduce | flops 7462 | bytes 59696 | tf_op jit(solution)/shard_map/psum | solution.py:296
  763.8 6.4 fusion.19
  770.2 103.1 %reduce-scatter.7.cloned.1.call-done = f32[192,2,768]{2,0,1:T(8,128)} async-done(((f32[1536,2,768]{2,0,1:T(8,128)}), f32[192,2,768]{2,0,1:T(8,128)}) %reduce-scatter.7.cloned.1.call-update) | async-done | bytes 1179664 | tf_op jit(solution)/shard_map/reduce_scatter | solution.py:310
  873.2 3.2 copy.469
  876.4 65.6 %reduce-scatter.9.cloned.1.call-done = f32[192,256]{1,0:T(8,128)} async-done(((f32[1536,256]{1,0:T(8,128)}), f32[192,256]{1,0:T(8,128)}) %reduce-scatter.9.cloned.1.call-update) | async-done | bytes 196624 | tf_op jit(solution)/shard_map/reduce_scatter | solution.py:311
  942.1 98.7 %reduce-scatter.11.cloned.1.call-done = f32[768,192]{0,1:T(8,128)} async-done(((f32[768,1536]{0,1:T(8,128)}), f32[768,192]{0,1:T(8,128)}) %reduce-scatter.11.cloned.1.call-update) | async-done | bytes 589840 | tf_op jit(solution)/shard_map/reduce_scatter | solution.py:188
  (360 shorter events, 117.4 us)
Async XLA Ops:
  7.2 4.9 copy-start.75
  7.2 19.9 %copy-start.85 = (f32[12]{0:T(128)S(1)}, f32[12]{0:T(128)}, u32[]{:S(2)}) copy-start(f32[12]{0:T(128)} %param.29) | copy-start | bytes 148
  7.2 19.9 %copy-start.50 = (f32[1536]{0:T(1024)S(1)}, f32[1536]{0:T(1024)}, u32[]{:S(2)}) copy-start(f32[1536]{0:T(1024)} %param.22) | copy-start | bytes 18436
  7.2 107.2 %all-gather.6.cloned.1.call-start = ((), (), s32[]{:S(2)}) async-start(), calls=%async_computation.4 | async-start | bytes 5898240 | tf_op jit(solution)/shard_map/all_gather | solution.py:94
  7.9 240.6 %all-gather.8.cloned.1.call-start = ((), (), s32[]{:S(2)}) async-start(), calls=%async_computation.5 | async-start | bytes 2949120 | tf_op jit(solution)/shard_map/all_gather | solution.py:97
  8.7 407.7 %all-reduce.6.cloned.1.call-start = ((), (), s32[]{:S(2)}) async-start(), calls=%async_computation.6 | async-start | bytes 2097152 | tf_op jit(solution)/shard_map/psum | solution.py:258
  8.7 18.4 %copy-start.3 = (bf16[1,1024,1536]{2,1,0:T(8,128)(2,1)S(1)}, bf16[1,1024,1536]{2,1,0:T(8,128)(2,1)}, u32[]{:S(2)}) copy-start(bf16[1,1024,1536]{2,1,0:T(8,128)(2,1)} %param.21) | copy-start | bytes 9437188
  12.1 105.7 %copy-start.62 = (f32[1024]{0:T(1024)}, f32[1024]{0:T(1024)S(1)}, u32[]{:S(2)}) copy-start(f32[1024]{0:T(1024)S(1)} %get-tuple-element.803) | copy-start | bytes 12292
  28.0 33.7 %copy-start.1 = (bf16[1024,1536]{1,0:T(8,128)(2,1)}, bf16[1024,1536]{1,0:T(8,128)(2,1)S(1)}, u32[]{:S(2)}) copy-start(bf16[1024,1536]{1,0:T(8,128)(2,1)S(1)} %fusion.16) | copy-start | bytes 9437188
  29.7 34.0 %copy-start.40 = (f32[1,4,256,12]{2,1,3,0:T(4,128)}, f32[1,4,256,12]{2,1,3,0:T(4,128)S(1)}, u32[]{:S(2)}) copy-start(f32[1,4,256,12]{2,1,3,0:T(4,128)S(1)} %reshape.676) | copy-start | bytes 147460
  65.4 52.4 %copy-start.31 = (f32[1,4,256,12]{2,1,3,0:T(4,128)}, f32[1,4,256,12]{2,1,3,0:T(4,128)S(1)}, u32[]{:S(2)}) copy-start(f32[1,4,256,12]{2,1,3,0:T(4,128)S(1)} %get-tuple-element.778) | copy-start | bytes 147460
  66.8 82.1 %copy-start.34 = (f32[1,4,256,12]{2,1,3,0:T(4,128)}, f32[1,4,256,12]{2,1,3,0:T(4,128)S(1)}, u32[]{:S(2)}) copy-start(f32[1,4,256,12]{2,1,3,0:T(4,128)S(1)} %reshape.682) | copy-start | bytes 147460
  117.8 5.1 copy-start.23
  129.0 22.0 %collective-permute-start = (f32[1,3,1024]{2,1,0:T(4,128)}, f32[1,3,1024]{2,1,0:T(4,128)S(1)}, u32[]{:S(2)}, u32[]{:S(2)}) collective-permute-start(f32[1,3,1024]{2,1,0:T(4,128)} %slice.128), channel_id=1, source_target_pairs={{0,4},{1,5},{2,6},{3,7},{8,12},{9,13},{10,14},{11,15},{16,20},{17,... | collective-permute-start | bytes 36872 | tf_op jit(solution)/shard_map/ppermute | solution.py:14
  151.0 10.0 copy-start.64
  164.6 6.6 copy-start.25
  164.7 6.6 copy-start.56
  196.5 15.7 %copy-start.45 = (f32[256,256]{1,0:T(8,128)S(1)}, f32[256,256]{1,0:T(8,128)}, u32[]{:S(2)}) copy-start(f32[256,256]{1,0:T(8,128)} %get-tuple-element.813) | copy-start | bytes 786436
  196.5 15.7 %copy-start.52 = (pred[256,256]{1,0:T(8,128)(4,1)S(1)}, pred[256,256]{1,0:T(8,128)(4,1)}, u32[]{:S(2)}) copy-start(pred[256,256]{1,0:T(8,128)(4,1)} %get-tuple-element.812) | copy-start | bytes 196612
  196.5 15.7 %copy-start.58 = (f32[4,12,256]{2,1,0:T(8,128)S(1)}, f32[4,12,256]{2,1,0:T(8,128)}, u32[]{:S(2)}) copy-start(f32[4,12,256]{2,1,0:T(8,128)} %copy.408) | copy-start | bytes 147460
  196.5 15.7 %copy-start.60 = (f32[4,12,256]{2,1,0:T(8,128)S(1)}, f32[4,12,256]{2,1,0:T(8,128)}, u32[]{:S(2)}) copy-start(f32[4,12,256]{2,1,0:T(8,128)} %copy.410) | copy-start | bytes 147460
  212.2 6.7 copy-start.6
  237.5 11.1 %copy-start.80 = (f32[768]{0:T(1024)S(1)}, f32[768]{0:T(1024)}, u32[]{:S(2)}) copy-start(f32[768]{0:T(1024)} %param.31) | copy-start | bytes 9220
  248.5 15.4 %copy-start.72 = (f32[1024]{0:T(1024)}, f32[1024]{0:T(1024)S(1)}, u32[]{:S(2)}) copy-start(f32[1024]{0:T(1024)S(1)} %get-tuple-element.805) | copy-start | bytes 12292
  274.5 7.0 copy-start.28
  274.5 7.0 copy-start.43
  313.5 5.3 copy-start.57
  323.0 11.9 %copy-start.17 = (bf16[1,1024,128]{2,1,0:T(8,128)(2,1)S(1)}, bf16[1,1024,128]{2,1,0:T(8,128)(2,1)}, u32[]{:S(2)}) copy-start(bf16[1,1024,128]{2,1,0:T(8,128)(2,1)} %get-tuple-element.788) | copy-start | bytes 786436
  323.0 12.0 %copy-start.69 = (f32[4,12]{1,0:T(4,128)S(1)}, f32[4,12]{1,0:T(4,128)}, u32[]{:S(2)}) copy-start(f32[4,12]{1,0:T(4,128)} %get-tuple-element.806) | copy-start | bytes 580
  323.0 12.0 %copy-start.70 = (f32[4,12]{1,0:T(4,128)S(1)}, f32[4,12]{1,0:T(4,128)}, u32[]{:S(2)}) copy-start(f32[4,12]{1,0:T(4,128)} %get-tuple-element.807) | copy-start | bytes 580
  343.3 14.2 %copy-start.12 = (f32[1024,768]{0,1:T(8,128)S(1)}, f32[1024,768]{0,1:T(8,128)}, u32[]{:S(2)}) copy-start(f32[1024,768]{0,1:T(8,128)} %copy.433) | copy-start | bytes 9437188
  372.8 4.7 copy-start.24
  372.8 4.7 copy-start.37
  378.6 6.6 copy-start.47
  378.6 7.7 copy-start.48
  378.6 8.7 copy-start.41
  378.6 8.7 copy-start.78
  378.6 9.9 copy-start.42
  378.6 10.0 copy-start.2
  381.9 101.3 %reduce-scatter.13.cloned.1.call-start = ((), (), s32[]{:S(2)}) async-start(), calls=%async_computation.10 | async-start | bytes 884736
  388.7 27.8 %copy-start.65 = (f32[1,3,1024]{2,1,0:T(4,128)S(1)}, f32[1,3,1024]{2,1,0:T(4,128)}, u32[]{:S(2)}) copy-start(f32[1,3,1024]{2,1,0:T(4,128)} %copy-done.64) | copy-start | bytes 36868
  390.6 315.5 %all-reduce.8.cloned.1.call-start = ((), (), s32[]{:S(2)}) async-start(), calls=%async_computation.11 | async-start | bytes 25165824 | tf_op jit(solution)/shard_map/psum | solution.py:181
  416.4 13.3 %copy-start.14 = (f32[1024,768]{1,0:T(8,128)S(1)}, f32[1024,768]{1,0:T(8,128)}, u32[]{:S(2)}) copy-start(f32[1024,768]{1,0:T(8,128)} %get-tuple-element.776) | copy-start | bytes 9437188
  416.4 13.3 %copy-start.73 = (f32[1024]{0:T(1024)S(1)}, f32[1024]{0:T(1024)}, u32[]{:S(2)}) copy-start(f32[1024]{0:T(1024)} %copy-done.72) | copy-start | bytes 12292
  416.4 13.3 %copy-start.81 = (f32[768]{0:T(1024)S(1)}, f32[768]{0:T(1024)}, u32[]{:S(2)}) copy-start(f32[768]{0:T(1024)} %param.31) | copy-start | bytes 9220
  416.4 13.3 %copy-start.84 = (bf16[768,1536]{1,0:T(8,128)(2,1)S(1)}, bf16[768,1536]{1,0:T(8,128)(2,1)}, u32[]{:S(2)}) copy-start(bf16[768,1536]{1,0:T(8,128)(2,1)} %all-gather.8.cloned.1.call-done) | copy-start | bytes 7077892
  416.4 22.2 %slice-start = ((s8[4718592]{0:T(1024)(128)(4,1)}), s8[4194304]{0:T(1024)(128)(4,1)S(1)}, s32[]{:S(2)}) async-start(s8[4718592]{0:T(1024)(128)(4,1)} %bitcast.347), calls=%async_computation.12 | async-start | bytes 8388608
  428.2 6.6 copy-start.66
  428.2 6.6 copy-start.67
  428.2 10.4 slice-start.1
  428.2 6.6 collective-permute-start.1
  438.6 6.9 copy-start.21
  440.4 5.1 copy-start.39
  449.2 424.0 %reduce-scatter.7.cloned.1.call-start = ((), (), s32[]{:S(2)}) async-start(), calls=%async_computation.7 | async-start | bytes 10616832 | tf_op jit(solution)/shard_map/reduce_scatter | solution.py:310
  453.1 4.7 copy-start.63
  468.3 473.8 %reduce-scatter.9.cloned.1.call-start = ((), (), s32[]{:S(2)}) async-start(), calls=%async_computation.8 | async-start | bytes 1769472 | tf_op jit(solution)/shard_map/reduce_scatter | solution.py:311
  471.5 569.3 %reduce-scatter.11.cloned.1.call-start = ((), (), s32[]{:S(2)}) async-start(), calls=%async_computation.9 | async-start | bytes 5308416 | tf_op jit(solution)/shard_map/reduce_scatter | solution.py:188
  484.8 225.6 %copy-start.49 = (f32[5,1024]{1,0:T(8,128)}, f32[5,1024]{1,0:T(8,128)S(1)}, u32[]{:S(2)}) copy-start(f32[5,1024]{1,0:T(8,128)S(1)} %stack.32) | copy-start | bytes 61444
  706.1 7.3 copy-start.18
  710.5 8.8 copy-start
  713.4 7.3 slice-start.2
  713.4 7.3 slice-start.3
  713.4 7.3 copy-start.79
  713.4 50.4 %copy-start.71 = (f32[1024]{0:T(1024)S(1)}, f32[1024]{0:T(1024)}, u32[]{:S(2)}) copy-start(f32[1024]{0:T(1024)} %get-tuple-element.802) | copy-start | bytes 12292
  (36 other events, 96.9 us)
Sparse Core Ops, SparseCore 0:
  9.6 104.7 all-gather.5
  116.0 48.6 all-gather.7
  382.0 34.3 all-reduce.5
  419.6 63.6 reduce-scatter.12
  486.2 219.8 all-reduce.7
  709.6 163.6 reduce-scatter.6
  877.2 64.8 reduce-scatter.8
  946.3 94.4 reduce-scatter.10
where the time goes:
time: 1060 us; the launch traced here: 1050 us
  waiting for transfers between devices  565 us (53%)
  local copies, waits for them, and re-layouts  125 us (12%)
  blocking collectives  125 us (12%)
  matrix products  111 us (10%)
  other arithmetic  99.2 us (9%)
  between operations  19.7 us (2%)
    psum x1, waiting for transfers between devices, on_device(): lax.psum(jnp.dot(out_in, out_full, preferred_element_type=jnp.float32), '...  221 us
    reduce_scatter x1, waiting for transfers between devices, on_device(): lax.psum_scatter(grad_wzx, ('shard', 'context'), scatter_dimension=0, til...  103 us
    reduce_scatter x1, waiting for transfers between devices, on_device(): lax.psum_scatter(grad_wout, ('shard', 'context'), scatter_dimension=1, ti...  98.7 us
    reduce_scatter x1, waiting for transfers between devices, on_device(): lax.psum_scatter(grad_wbc, ('shard', 'context'), scatter_dimension=0, til...  65.6 us
    all_gather x1, waiting for transfers between devices, on_device(): lax.all_gather(w_in_zx, 'shard', axis=0, tiled=True)  46.2 us
    psum x1, blocking collectives, on_device(): lax.psum((grad_ng, grad_taps[:, :inner_dev], grad_taps[:, inner_dev:], gr...  41.1 us
    all_gather x1, blocking collectives, on_device(): lax.all_gather(w_in_bc, 'shard', axis=0, tiled=True)  29.5 us
    psum x1, waiting for transfers between devices, on_device(): bc_sum = lax.psum(bc_part, 'tensor')  25.7 us
  transfers between devices with their start and end apart: 10, of which 7 were waited for; matrix products, arithmetic and copies ran while one was open for 20% of the time, Pallas kernels for 0%

commit v1 on v0

--- a/solution.py
+++ b/solution.py
@@ -6,6 +6,19 @@
 CH = 256
 EPSILON = 1e-05
 PRECISE = lax.Precision.HIGHEST
+
+
+def touch_cycles(here_x):
+    mesh_name = "tensor"
+    n_axis = lax.axis_size(mesh_name)
+    res, f_now = (here_x, 0)
+    while 1 << f_now < n_axis:
+        carry = lax.ppermute(
+            res, axis_name=mesh_name, perm=[(d, d ^ 1 << f_now) for d in range(n_axis)]
+        )
+        res = res + carry
+        f_now = f_now + 1
+    return res
 
 
 def shifted(array, axis, by):
@@ -255,7 +268,7 @@
     grad_raw = grad_dt_q.reshape(row_count, heads_dev) * jax.nn.sigmoid(dt_pre)
     grad_dtb = jnp.sum(grad_raw, axis=0)
     bc_part = jnp.concatenate([grad_bm, grad_cm], axis=-1).reshape(row_count, 2 * state_dim)
-    bc_sum = lax.psum(bc_part, "tensor")
+    bc_sum = touch_cycles(bc_part)
     grad_act = jnp.concatenate(
         [
             grad_xa.reshape(seq_count, local_len, inner_dev),

time: 1060 us -> 1020 us (0.962)
  waiting for transfers between devices: 565 us -> 529 us
    psum x1 -> x0, waiting for transfers between devices: 25.7 us -> none  [on_device(): bc_sum = lax.psum(bc_part, 'tensor')]
    psum x1, waiting for transfers between devices: 221 us -> 198 us  [on_device(): lax.psum(jnp.dot(out_in, out_full, preferred_element_type=jnp.float32), '...]
    ppermute x0 -> x2, waiting for transfers between devices: none -> 19.2 us  [touch_cycles(): lax.ppermute(res, axis_name=mesh_name, perm=[(d, d ^ 1 << f_now) for d in...]
    unnamed x186 -> x188, local copies, waits for them, and re-layouts: 23.9 us -> 22.5 us
  transfers between devices with their start and end apart: 10 -> 11, of which waited for: 7 -> 6; matrix products, arithmetic and copies ran while one was open for 20% -> 22% of each run, Pallas kernels for 0% -> 0%
where the time goes in v1:
time: 1020 us; the launch traced here: 1010 us
  waiting for transfers between devices  529 us (52%)
  blocking collectives  125 us (12%)
  matrix products  118 us (12%)
  local copies, waits for them, and re-layouts  116 us (11%)
  other arithmetic  98.2 us (10%)
  between operations  19.9 us (2%)
    psum x1, waiting for transfers between devices, on_device(): lax.psum(jnp.dot(out_in, out_full, preferred_element_type=jnp.float32), '...  198 us
    reduce_scatter x1, waiting for transfers between devices, on_device(): lax.psum_scatter(grad_wzx, ('shard', 'context'), scatter_dimension=0, til...  103 us
    reduce_scatter x1, waiting for transfers between devices, on_device(): lax.psum_scatter(grad_wout, ('shard', 'context'), scatter_dimension=1, ti...  98.7 us
    reduce_scatter x1, waiting for transfers between devices, on_device(): lax.psum_scatter(grad_wbc, ('shard', 'context'), scatter_dimension=0, til...  65.4 us
    all_gather x1, waiting for transfers between devices, on_device(): lax.all_gather(w_in_zx, 'shard', axis=0, tiled=True)  43.2 us
    psum x1, blocking collectives, on_device(): lax.psum((grad_ng, grad_taps[:, :inner_dev], grad_taps[:, inner_dev:], gr...  40.9 us
    all_gather x1, blocking collectives, on_device(): lax.all_gather(w_in_bc, 'shard', axis=0, tiled=True)  30.1 us
    unnamed x188, local copies, waits for them, and re-layouts  22.5 us
  transfers between devices with their start and end apart: 11, of which 6 were waited for; matrix products, arithmetic and copies ran while one was open for 22% of the time, Pallas kernels for 0%

profile of v1, /device:TPU:0, one launch (start us, length us, event | category | flops | bytes accessed | tf_op | source)
XLA Modules:
  0.0 1014.2 jit_solution(1849182805874339387)
XLA Ops:
  8.8 2.7 fusion.14
  12.1 15.0 %all_gather.34 = bf16[1536,12]{0,1:T(8,128)(2,1)S(1)} all-gather(bf16[384,12]{0,1:T(8,128)(2,1)S(1)} %copy-done.73), channel_id=1, replica_groups=mesh['shard'=4,'context'=2,'tensor'=4] {'shard'}, dimensions={0}, use_global_device_ids=true | all-gather | bytes 46080 | tf_op jit(solution)/shard_map/all_gather | solution.py:109
  33.8 30.1 %all_gather.33 = bf16[1536,256]{1,0:T(8,128)(2,1)S(1)} all-gather(bf16[384,256]{1,0:T(8,128)(2,1)S(1)} %copy-done.44), channel_id=1, replica_groups=mesh['shard'=4,'context'=2,'tensor'=4] {'shard'}, dimensions={0}, use_global_device_ids=true | all-gather | bytes 983040 | tf_op jit(solution)/shard_map/all_gather | solution.py:108
  63.9 3.2 fusion.130
  71.1 43.2 %all-gather.6.cloned.1.call-done = bf16[1536,2,768]{2,1,0:T(2,128)(2,1)} async-done(((bf16[384,2,768]{2,1,0:T(2,128)(2,1)}), bf16[1536,2,768]{2,1,0:T(2,128)(2,1)}) %all-gather.6.cloned.1.call-update) | async-done | bytes 4718608 | tf_op jit(solution)/shard_map/all_gather | solution.py:107
  114.4 3.4 copy.488
  117.9 5.1 fusion.61
  129.0 3.9 collective-permute-start
  139.3 5.4 all-reduce
  148.9 10.0 multiply_convert_fusion.3
  158.9 2.7 fusion.126
  162.5 2.7 copy.402
  165.2 3.8 reshape.673
  169.1 3.1 convolution_bitcast_fusion
  174.2 9.7 while.60
  188.3 3.6 copy.426
  191.9 5.2 reshape.700
  197.1 10.5 %all-gather.1 = f32[2,12,128,64]{2,3,1,0:T(8,128)} all-gather(f32[1,12,128,64]{2,3,1,0:T(8,128)S(1)} %copy.421), channel_id=3, replica_groups=mesh['shard'=4,'context'=2,'tensor'=4] {'context'}, dimensions={0}, use_global_device_ids=true | all-gather | bytes 1179648 | tf_op jit(solution)/shard_map/all_gather | solution.py:32
  207.6 6.7 fusion.32
  214.3 3.0 while.61
  217.3 6.0 bitcast_add_fusion.5
  227.9 3.5 copy.429
  231.4 5.4 multiply_reduce_fusion.10
  236.8 5.6 psum.84
  242.5 8.6 multiply_reduce_fusion.8
  251.0 6.7 psum.86
  257.8 7.4 fusion.52
  267.8 3.1 copy.433
  270.9 3.9 reshape.688
  274.8 4.4 fusion.73
  281.2 9.7 while.62
  291.2 10.7 %all-gather.2 = f32[2,12,128,64]{2,3,1,0:T(8,128)S(1)} all-gather(f32[1,12,128,64]{2,3,1,0:T(8,128)S(1)} %copy.438), channel_id=4, replica_groups=mesh['shard'=4,'context'=2,'tensor'=4] {'context'}, dimensions={0}, use_global_device_ids=true | all-gather | bytes 1179648 | tf_op jit(solution)/shard_map/all_gather | solution.py:32
  304.2 3.5 fusion.55
  310.2 4.0 fusion.77
  314.3 11.5 %fusion.12 = (f32[4,12,256]{2,1,0:T(8,128)}, f32[4,12,256]{2,1,0:T(8,128)}, f32[4,12,256]{2,1,0:T(8,128)}, f32[4,256,256]{2,1,0:T(8,128)S(1)}) fusion(f32[4,12,256]{2,1,0:T(8,128)S(1)} %copy-done.60, f32[256,256]{1,0:T(8,128)S(1)} %copy-done.43, f32[4,12,256]{2,1,0:T(8,128)S(1)} %copy-done.58, f32[4,256,256]{2,1,0:T(8,128)S(1)} %copy-done.31, ...), kind=kOutput, calls=%fused_computation.32 | convolution fusion | flops 446394368 | bytes 5816320 | tf_op jit(solution)/shard_map/scihp,scjhp->schij/dot_general | solution.py:211
  326.8 3.4 fusion.132
  330.2 5.2 reshape.701
  335.4 3.1 fusion.47
  339.2 7.7 fusion.51
  359.9 5.6 copy.442
  365.5 5.2 reshape.689
  370.7 3.5 copy.451
  374.3 3.8 fusion.54
  383.8 3.8 fusion.105
  387.6 19.2 %collective-permute-done.2 = f32[1024,256]{1,0:T(8,128)S(1)} collective-permute-done((f32[1024,256]{1,0:T(8,128)}, f32[1024,256]{1,0:T(8,128)S(1)}, u32[]{:S(2)}, u32[]{:S(2)}) %collective-permute-start.2) | collective-permute-done | bytes 1048608 | tf_op jit(solution)/shard_map/ppermute | solution.py:16
  408.3 11.2 %fusion.120 = (f32[1024]{0:T(1024)S(1)}, f32[1024]{0:T(1024)S(1)}, f32[1024]{0:T(1024)S(1)}, f32[1024]{0:T(1024)S(1)}, f32[1024]{0:T(1024)S(1)}, /*index=5*/f32[1,1024,1024]{2,1,0:T(8,128)S(1)}) fusion(f32[1024,256]{1,0:T(8,128)S(1)} %copy-done.14, f32[1024,768]{1,0:T(8,128)} %copy-done.8, f32[1,1024,1024]{2,1,0:T(8,128)} %copy-done.6, ...), kind=kLoop, calls=%fused_computation.209 | loop fusion | flops 23063552 | bytes 21004288 | tf_op jit(solution)/shard_map/reduce_sum | solution.py:290
  421.0 5.1 fusion.119
  430.4 5.1 fusion.70
  435.5 3.7 convolution_add_fusion.1
  439.2 3.9 fusion.69
  443.1 4.7 copy.481
  447.8 10.4 %fusion.49 = f32[1536,2,768]{2,0,1:T(8,128)} fusion(bf16[2,768,1024]{2,1,0:T(8,128)(2,1)} %bitcast.359, bf16[1,1024,1536]{2,1,0:T(8,128)(2,1)} %param.21, f32[1536]{0:T(1024)S(1)} %copy-done.49, f32[1024]{0:T(1024)S(1)} %copy-done.64), kind=kOutput, calls=%fused_computation.92 | convolution fusion | flops 4838129664 | bytes 15738880 | tf_op jit(solution)/shard_map/dot_general | solution.py:57
  458.2 4.1 fusion.92
  462.6 7.8 fusion.56
  472.3 198.1 %all-reduce.5.cloned.1.call-done = (f32[1024,1536]{1,0:T(8,128)}, f32[1024,1536]{1,0:T(8,128)}) async-done(((f32[1024,1536]{1,0:T(8,128)}, f32[1024,1536]{1,0:T(8,128)}), (f32[1024,1536]{1,0:T(8,128)}, f32[1024,1536]{1,0:T(8,128)})) %all-reduce.5.cloned.1.call-update) | async-done | bytes 12582928 | tf_op jit(solution)/shard_map/psum | solution.py:194
  670.5 4.0 convolution_add_fusion
  674.5 3.0 copy-done.16
  677.4 5.9 multiply_reduce_fusion.3
  684.7 40.9 %all-reduce.1 = (f32[1536]{0:T(1024)}, f32[5,768]{1,0:T(8,128)}, f32[5,256]{1,0:T(8,128)}, f32[12]{0:T(128)}, f32[12]{0:T(128)}, /*index=5*/f32[12]{0:T(128)}, f32[768]{0:T(1024)}, f32[2]{0:T(128)S(1)}) all-reduce(f32[1536]{0:T(1024)S(1)} %get-tuple-element.717, ...), channel_id=1, replica_groups=mesh['shard'=4,'context'=2,'tensor'=4] {'shard','context'}, use_global_device_ids=true, to_apply=%region_33.34 | all-reduce | flops 7462 | bytes 59696 | tf_op jit(solution)/shard_map/psum | solution.py:309
  727.6 7.3 fusion.19
  734.9 102.6 %reduce-scatter.7.cloned.1.call-done = f32[192,2,768]{2,0,1:T(8,128)} async-done(((f32[1536,2,768]{2,0,1:T(8,128)}), f32[192,2,768]{2,0,1:T(8,128)}) %reduce-scatter.7.cloned.1.call-update) | async-done | bytes 1179664 | tf_op jit(solution)/shard_map/reduce_scatter | solution.py:323
  837.6 3.2 copy.469
  840.8 65.4 %reduce-scatter.9.cloned.1.call-done = f32[192,256]{1,0:T(8,128)} async-done(((f32[1536,256]{1,0:T(8,128)}), f32[192,256]{1,0:T(8,128)}) %reduce-scatter.9.cloned.1.call-update) | async-done | bytes 196624 | tf_op jit(solution)/shard_map/reduce_scatter | solution.py:324
  906.2 98.7 %reduce-scatter.11.cloned.1.call-done = f32[768,192]{0,1:T(8,128)} async-done(((f32[768,1536]{0,1:T(8,128)}), f32[768,192]{0,1:T(8,128)}) %reduce-scatter.11.cloned.1.call-update) | async-done | bytes 589840 | tf_op jit(solution)/shard_map/reduce_scatter | solution.py:201
  (365 shorter events, 105.7 us)
Async XLA Ops:
  7.2 19.9 %copy-start.85 = (f32[12]{0:T(128)S(1)}, f32[12]{0:T(128)}, u32[]{:S(2)}) copy-start(f32[12]{0:T(128)} %param.29) | copy-start | bytes 148
  7.2 19.9 %copy-start.48 = (f32[1536]{0:T(1024)S(1)}, f32[1536]{0:T(1024)}, u32[]{:S(2)}) copy-start(f32[1536]{0:T(1024)} %param.22) | copy-start | bytes 18436
  7.2 107.2 %all-gather.6.cloned.1.call-start = ((), (), s32[]{:S(2)}) async-start(), calls=%async_computation.4 | async-start | bytes 5898240 | tf_op jit(solution)/shard_map/all_gather | solution.py:107
  7.9 234.5 %all-gather.8.cloned.1.call-start = ((), (), s32[]{:S(2)}) async-start(), calls=%async_computation.5 | async-start | bytes 2949120 | tf_op jit(solution)/shard_map/all_gather | solution.py:110
  8.7 462.0 %reduce-scatter.13.cloned.1.call-start = ((), (), s32[]{:S(2)}) async-start(), calls=%async_computation.9 | async-start | bytes 884736
  8.7 18.4 %copy-start.2 = (bf16[1,1024,1536]{2,1,0:T(8,128)(2,1)S(1)}, bf16[1,1024,1536]{2,1,0:T(8,128)(2,1)}, u32[]{:S(2)}) copy-start(bf16[1,1024,1536]{2,1,0:T(8,128)(2,1)} %param.21) | copy-start | bytes 9437188
  12.1 105.8 %copy-start.63 = (f32[1024]{0:T(1024)}, f32[1024]{0:T(1024)S(1)}, u32[]{:S(2)}) copy-start(f32[1024]{0:T(1024)S(1)} %get-tuple-element.803) | copy-start | bytes 12292
  67.1 81.8 %copy-start.13 = (f32[1024,256]{1,0:T(8,128)}, f32[1024,256]{1,0:T(8,128)S(1)}, u32[]{:S(2)}) copy-start(f32[1024,256]{1,0:T(8,128)S(1)} %fusion.130) | copy-start | bytes 3145732
  68.9 48.9 %copy-start.29 = (f32[1,4,256,12]{2,1,3,0:T(4,128)}, f32[1,4,256,12]{2,1,3,0:T(4,128)S(1)}, u32[]{:S(2)}) copy-start(f32[1,4,256,12]{2,1,3,0:T(4,128)S(1)} %get-tuple-element.778) | copy-start | bytes 147460
  70.4 47.5 %copy-start.45 = (f32[4,12]{0,1:T(8,128)}, f32[4,12]{0,1:T(8,128)S(1)}, u32[]{:S(2)}) copy-start(f32[4,12]{0,1:T(8,128)S(1)} %copy.417) | copy-start | bytes 580
  70.4 76.4 %copy-start.32 = (f32[1,4,256,12]{2,1,3,0:T(4,128)}, f32[1,4,256,12]{2,1,3,0:T(4,128)S(1)}, u32[]{:S(2)}) copy-start(f32[1,4,256,12]{2,1,3,0:T(4,128)S(1)} %reshape.682) | copy-start | bytes 147460
  129.0 19.9 %collective-permute-start = (f32[1,3,1024]{2,1,0:T(4,128)}, f32[1,3,1024]{2,1,0:T(4,128)}, u32[]{:S(2)}, u32[]{:S(2)}) collective-permute-start(f32[1,3,1024]{2,1,0:T(4,128)} %slice.128), channel_id=1, source_target_pairs={{0,4},{1,5},{2,6},{3,7},{8,12},{9,13},{10,14},{11,15},{16,20},{17,... | collective-permute-start | bytes 36872 | tf_op jit(solution)/shard_map/ppermute | solution.py:27
  162.5 6.6 copy-start.22
  162.5 6.6 copy-start.55
  191.8 15.7 %copy-start.42 = (f32[256,256]{1,0:T(8,128)S(1)}, f32[256,256]{1,0:T(8,128)}, u32[]{:S(2)}) copy-start(f32[256,256]{1,0:T(8,128)} %get-tuple-element.813) | copy-start | bytes 786436
  191.8 15.7 %copy-start.50 = (pred[256,256]{1,0:T(8,128)(4,1)S(1)}, pred[256,256]{1,0:T(8,128)(4,1)}, u32[]{:S(2)}) copy-start(pred[256,256]{1,0:T(8,128)(4,1)} %get-tuple-element.812) | copy-start | bytes 196612
  191.8 15.7 %copy-start.57 = (f32[4,12,256]{2,1,0:T(8,128)S(1)}, f32[4,12,256]{2,1,0:T(8,128)}, u32[]{:S(2)}) copy-start(f32[4,12,256]{2,1,0:T(8,128)} %copy.408) | copy-start | bytes 147460
  191.9 15.7 %copy-start.59 = (f32[4,12,256]{2,1,0:T(8,128)S(1)}, f32[4,12,256]{2,1,0:T(8,128)}, u32[]{:S(2)}) copy-start(f32[4,12,256]{2,1,0:T(8,128)} %copy.410) | copy-start | bytes 147460
  207.6 6.7 copy-start.5
  207.6 6.7 copy-start.86
  231.4 11.0 %copy-start.78 = (f32[768]{0:T(1024)S(1)}, f32[768]{0:T(1024)}, u32[]{:S(2)}) copy-start(f32[768]{0:T(1024)} %param.31) | copy-start | bytes 9220
  267.8 7.0 copy-start.26
  267.8 7.0 copy-start.40
  304.2 5.9 copy-start.56
  314.3 11.5 %copy-start.15 = (bf16[1,1024,128]{2,1,0:T(8,128)(2,1)S(1)}, bf16[1,1024,128]{2,1,0:T(8,128)(2,1)}, u32[]{:S(2)}) copy-start(bf16[1,1024,128]{2,1,0:T(8,128)(2,1)} %get-tuple-element.788) | copy-start | bytes 786436
  314.3 12.6 %copy-start.23 = (bf16[1,1024,128]{2,1,0:T(8,128)(2,1)S(1)}, bf16[1,1024,128]{2,1,0:T(8,128)(2,1)}, u32[]{:S(2)}) copy-start(bf16[1,1024,128]{2,1,0:T(8,128)(2,1)} %copy-done.22) | copy-start | bytes 786436
  325.8 25.6 %copy-start.21 = (f32[4,256,256]{2,1,0:T(8,128)}, f32[4,256,256]{2,1,0:T(8,128)S(1)}, u32[]{:S(2)}) copy-start(f32[4,256,256]{2,1,0:T(8,128)S(1)} %get-tuple-element.699) | copy-start | bytes 3145732
  339.2 7.7 copy-start.7
  339.2 7.7 copy-start.34
  339.2 7.7 copy-start.41
  351.4 5.3 copy-start.53
  351.4 5.3 copy-start.54
  351.4 5.3 copy-start.30
  351.4 5.3 copy-start.33
  351.4 5.3 copy-start.46
  351.4 5.3 copy-start.62
  356.7 22.1 %collective-permute-start.1 = (f32[1024,256]{1,0:T(8,128)}, f32[1024,256]{1,0:T(8,128)}, u32[]{:S(2)}, u32[]{:S(2)}) collective-permute-start(f32[1024,256]{1,0:T(8,128)} %pad_maximum_fusion.4), channel_id=1, source_target_pairs={{0,1},{1,0},{2,3},{3,2},{4,5},{5,4},{6,7},{7,6},{8,9},{9,8},{10,11... | collective-permute-start | bytes 3145736 | tf_op jit(solution)/shard_map/ppermute | solution.py:16
  378.0 5.3 copy-start.76
  378.0 5.6 copy-start.39
  381.1 25.8 %collective-permute-start.2 = (f32[1024,256]{1,0:T(8,128)}, f32[1024,256]{1,0:T(8,128)S(1)}, u32[]{:S(2)}, u32[]{:S(2)}) collective-permute-start(f32[1024,256]{1,0:T(8,128)} %fusion.118), channel_id=1, source_target_pairs={{0,2},{1,3},{2,0},{3,1},{4,6},{5,7},{6,4},{7,5},{8,10},{9,11},{10,... | collective-permute-start | bytes 3145736 | tf_op jit(solution)/shard_map/ppermute | solution.py:16
  387.6 20.7 %copy-start.14 = (f32[1024,256]{1,0:T(8,128)S(1)}, f32[1024,256]{1,0:T(8,128)}, u32[]{:S(2)}) copy-start(f32[1024,256]{1,0:T(8,128)} %copy-done.13) | copy-start | bytes 3145732
  387.6 282.9 %all-reduce.5.cloned.1.call-start = ((), (), s32[]{:S(2)}) async-start(), calls=%async_computation.10 | async-start | bytes 25165824 | tf_op jit(solution)/shard_map/psum | solution.py:194
  408.2 12.7 %copy-start.12 = (f32[1024,768]{1,0:T(8,128)S(1)}, f32[1024,768]{1,0:T(8,128)}, u32[]{:S(2)}) copy-start(f32[1024,768]{1,0:T(8,128)} %get-tuple-element.776) | copy-start | bytes 9437188
  408.2 12.7 %copy-start.79 = (f32[768]{0:T(1024)S(1)}, f32[768]{0:T(1024)}, u32[]{:S(2)}) copy-start(f32[768]{0:T(1024)} %param.31) | copy-start | bytes 9220
  408.2 12.7 %copy-start.84 = (bf16[768,1536]{1,0:T(8,128)(2,1)S(1)}, bf16[768,1536]{1,0:T(8,128)(2,1)}, u32[]{:S(2)}) copy-start(bf16[768,1536]{1,0:T(8,128)(2,1)} %all-gather.8.cloned.1.call-done) | copy-start | bytes 7077892
  408.3 20.3 %slice-start = ((s8[4718592]{0:T(1024)(128)(4,1)}), s8[4194304]{0:T(1024)(128)(4,1)S(1)}, s32[]{:S(2)}) async-start(s8[4718592]{0:T(1024)(128)(4,1)} %bitcast.347), calls=%async_computation.11 | async-start | bytes 8388608
  419.4 6.6 copy-start.65
  419.5 6.6 copy-start.66
  419.5 6.6 copy-start.67
  419.5 6.6 copy-start.68
  419.5 9.1 slice-start.1
  419.5 6.6 collective-permute-start.3
  428.6 6.9 copy-start.18
  439.2 398.4 %reduce-scatter.7.cloned.1.call-start = ((), (), s32[]{:S(2)}) async-start(), calls=%async_computation.6 | async-start | bytes 10616832 | tf_op jit(solution)/shard_map/reduce_scatter | solution.py:323
  458.2 448.0 %reduce-scatter.9.cloned.1.call-start = ((), (), s32[]{:S(2)}) async-start(), calls=%async_computation.7 | async-start | bytes 1769472 | tf_op jit(solution)/shard_map/reduce_scatter | solution.py:324
  462.4 542.5 %reduce-scatter.11.cloned.1.call-start = ((), (), s32[]{:S(2)}) async-start(), calls=%async_computation.8 | async-start | bytes 5308416 | tf_op jit(solution)/shard_map/reduce_scatter | solution.py:201
  470.4 200.0 %copy-start.25 = (bf16[1536,256]{1,0:T(8,128)(2,1)S(1)}, bf16[1536,256]{1,0:T(8,128)(2,1)}, u32[]{:S(2)}) copy-start(bf16[1536,256]{1,0:T(8,128)(2,1)} %copy-done.24) | copy-start | bytes 2359300
  472.3 202.1 %copy-start.47 = (f32[5,1024]{1,0:T(8,128)}, f32[5,1024]{1,0:T(8,128)S(1)}, u32[]{:S(2)}) copy-start(f32[5,1024]{1,0:T(8,128)S(1)} %stack.32) | copy-start | bytes 61444
  670.5 7.0 copy-start.16
  674.4 8.9 copy-start
  677.4 7.2 slice-start.2
  677.4 7.2 slice-start.3
  677.4 7.2 copy-start.77
  677.4 50.2 %copy-start.72 = (f32[1024]{0:T(1024)S(1)}, f32[1024]{0:T(1024)}, u32[]{:S(2)}) copy-start(f32[1024]{0:T(1024)} %get-tuple-element.802) | copy-start | bytes 12292
  (38 other events, 136.0 us)
Sparse Core Ops, SparseCore 0:
  9.6 104.7 all-gather.5
  116.0 48.6 all-gather.7
  387.7 59.9 reduce-scatter.12
  450.7 219.6 all-reduce.4
  673.9 163.6 reduce-scatter.6
  841.4 64.7 reduce-scatter.8
  910.4 94.4 reduce-scatter.10
